TPU v7x, 32 devices: a whole 2x2x4 slice. The times are simulated.
32 devices in a mesh: fsdp: 8 (over y, x, core), cp: 4 (over z).
Axes of the slice: x: 2, y: 2, z: 4, core: 2. Of those that a mesh axis runs over, the one named last changes fastest.
Arguments:
- features: bfloat16 [8, 512, 2560], P('fsdp', 'cp'), may hold values from -6 to 6
- query_rows: bfloat16 [8, 512, 1280], P('fsdp', 'cp'), may hold values from -40 to 40, as said below
- key_rows: bfloat16 [8, 512, 1280], P('fsdp', 'cp'), may hold values from -4 to 4
- value_rows: bfloat16 [8, 512, 1280], P('fsdp', 'cp'), may hold values from -6 to 6
- attn_output: bfloat16 [8, 512, 1280], P('fsdp', 'cp'), may hold values from -6 to 6
- grad_output: bfloat16 [8, 512, 1280], P('fsdp', 'cp'), may hold values from -6 to 6
- log_sums: float32 [8, 512, 10], P('fsdp', 'cp'), as said below
Outputs:
- d_query: bfloat16 [8, 512, 1280], P('fsdp', 'cp')
- d_key: bfloat16 [8, 512, 1280], P('fsdp', 'cp')
- d_value: bfloat16 [8, 512, 1280], P('fsdp', 'cp')
- d_value_weight: float32 [2560, 1280], P('fsdp', 'cp')
Inputs may be any that keep to these rules, and one draw needn't show every extreme that they name: `query_rows`: queries of a clip, with key_rows and log_sums drawn together with them. log_sums[c, t, h] is the logarithm of the sum over all 512 keys u of clip c of exp(128**-0.5 * q[t] . k[u]) for head h, computed from the bfloat16 queries and keys in float32.
All inputs are finite; a program needn't handle non-finite values.
Results may differ from a plain program's by a relative error of at most 0.02.
Values may be sent and summed in bfloat16 or wider, within the bound.
No kernel may reach another device: no remote copies, remote signals or barrier semaphores. Data moves between devices by JAX's collectives and lax.ppermute only.
A program may use at most 128 MiB of HBM per device.

v0:
```python
import jax
import jax.numpy as jnp
from jax import lax
from jax.sharding import PartitionSpec as P


def passed_along(value, axis, steps):
    count = lax.axis_size(axis)
    pairs = [(source, (source + steps) % count) for source in range(count)]
    return lax.ppermute(value, axis, pairs)


def on_device(features, query_rows, key_rows, value_rows, attn_output, grad_output, log_sums):
    rows_here = query_rows.shape[1]
    proj_width = query_rows.shape[2]
    head_count = log_sums.shape[2]
    head_size = proj_width // head_count
    softmax_scale = head_size ** (-0.5)

    def as_heads(block):
        return block[0].reshape(block.shape[1], head_count, head_size)

    product = grad_output.astype(jnp.float32) * attn_output.astype(jnp.float32)
    row_delta = jnp.sum(product.reshape(1, rows_here, head_count, head_size), axis=3)
    own_key = as_heads(key_rows)
    own_value = as_heads(value_rows)
    all_norms, all_deltas = (
        lax.all_gather(log_sums, "cp", axis=1, tiled=True),
        lax.all_gather(row_delta, "cp", axis=1, tiled=True),
    )

    def pair_scores(query_heads, grad_heads, offset, rows_in):
        norm_block = lax.dynamic_slice_in_dim(all_norms, offset, rows_in, 1)[0].T
        delta_block = lax.dynamic_slice_in_dim(all_deltas, offset, rows_in, 1)[0].T
        scores = (
            jnp.einsum("qhd,khd->hqk", query_heads, own_key, preferred_element_type=jnp.float32)
            * softmax_scale
        )
        attn_prob = jnp.exp(scores - norm_block[:, :, None])
        grad_prob = jnp.einsum(
            "qhd,khd->hqk", grad_heads, own_value, preferred_element_type=jnp.float32
        )
        grad_score = (attn_prob * (grad_prob - delta_block[:, :, None])).astype(jnp.bfloat16)
        return (grad_score, attn_prob.astype(jnp.bfloat16))

    zero_rows = jnp.zeros((rows_here, head_count, head_size), jnp.float32)
    position = lax.axis_index("cp")
    cycle_count = lax.axis_size("cp")

    def cycle_step(step, state):
        query_block, grad_block, query_run, key_run, value_run = state
        source = (position - step) % cycle_count
        offset = source * rows_here
        query_heads = as_heads(query_block)
        grad_heads = as_heads(grad_block)
        grad_score, prob_half = pair_scores(query_heads, grad_heads, offset, rows_here)
        query_run = query_run + jnp.einsum(
            "hqk,khd->qhd", grad_score, own_key, preferred_element_type=jnp.float32
        )
        key_run = key_run + jnp.einsum(
            "hqk,qhd->khd", grad_score, query_heads, preferred_element_type=jnp.float32
        )
        value_run = value_run + jnp.einsum(
            "hqk,qhd->khd", prob_half, grad_heads, preferred_element_type=jnp.float32
        )
        query_block, grad_block = passed_along((query_block, grad_block), "cp", 1)
        query_run = passed_along(query_run.astype(jnp.bfloat16), "cp", 1).astype(query_run.dtype)
        return (query_block, grad_block, query_run, key_run, value_run)

    start_state = (query_rows, grad_output, zero_rows, zero_rows, zero_rows)
    final_state = lax.fori_loop(0, cycle_count, cycle_step, start_state)
    query_total, key_total, value_total = (final_state[2], final_state[3], final_state[4])
    d_query = (softmax_scale * query_total).astype(jnp.bfloat16).reshape(1, rows_here, proj_width)
    d_key = (softmax_scale * key_total).astype(jnp.bfloat16).reshape(1, rows_here, proj_width)
    d_value = value_total.astype(jnp.bfloat16).reshape(1, rows_here, proj_width)
    feature_cols = features[0]
    row_sums = lax.psum_scatter(
        jnp.einsum(
            "tf,tw->fw", feature_cols, d_value[0], preferred_element_type=jnp.float32
        ).astype(jnp.bfloat16),
        "fsdp",
        scatter_dimension=0,
        tiled=True,
    )
    weight_part = lax.psum_scatter(row_sums, "cp", scatter_dimension=1, tiled=True).astype(
        jnp.float32
    )
    return (d_query, d_key, d_value, weight_part)


def solution(mesh):
    return jax.shard_map(
        on_device,
        mesh=mesh,
        in_specs=(
            P("fsdp", "cp", None),
            P("fsdp", "cp", None),
            P("fsdp", "cp", None),
            P("fsdp", "cp", None),
            P("fsdp", "cp", None),
            P("fsdp", "cp", None),
            P("fsdp", "cp", None),
        ),
        out_specs=(
            P("fsdp", "cp", None),
            P("fsdp", "cp", None),
            P("fsdp", "cp", None),
            P("fsdp", "cp"),
        ),
        check_vma=False,
    )
```

profile of v0, /device:TPU:0, one launch (start us, length us, event | category | flops | bytes accessed | tf_op | source)
XLA Modules:
  0.0 243.9 jit_solution(6406590973211021745)
XLA Ops:
  8.0 14.8 %all_gather.6 = f32[1,512,10]{1,2,0:T(8,128)S(1)} all-gather(f32[1,128,10]{1,2,0:T(8,128)S(1)} %copy.51), channel_id=1, replica_groups=mesh['fsdp'=8,'cp'=4] {'cp'}, dimensions={1}, use_global_device_ids=true | all-gather | bytes 25600 | tf_op jit(solution)/shard_map/all_gather | solution.py:28
  24.0 1.9 copy.55
  30.7 13.1 %all-gather = f32[512,10]{0,1:T(8,128)S(1)} all-gather(f32[128,10]{0,1:T(8,128)S(1)} %reduce_sum.11), channel_id=2, replica_groups=mesh['fsdp'=8,'cp'=4] {'cp'}, dimensions={0}, use_global_device_ids=true | all-gather | bytes 25600 | tf_op jit(solution)/shard_map/all_gather | solution.py:29
  43.8 87.0 %while.24 = (s32[]{:T(128)}, bf16[1,128,1280]{1,2,0:T(8,128)(2,1)}, bf16[1,128,1280]{1,2,0:T(8,128)(2,1)S(1)}, f32[128,10,128]{2,0,1:T(8,128)}, f32[128,10,128]{...) while((s32[]{:T(128)}, bf16[1,128,1280]{1,2,0:T(8,128)(2,1)}, ...), condition=%wide.region_2.3_spmd.clone, body=%wide.region_1.2_spmd.clone.sunk | while | flops 212008976 | bytes 15104460 | solution.py:71
  44.8 1.6 collective-permute-start
  46.9 1.4 fusion.47
  49.2 2.9 %collective-permute-start.2 = (bf16[128,10,128]{2,0,1:T(8,128)(2,1)}, bf16[128,10,128]{2,0,1:T(8,128)(2,1)}, u32[]{:S(2)}, u32[]{:S(2)}) collective-permute-start(bf16[128,10,128]{2,0,1:T(8,128)(2,1)} %fusion.48), channel_id=1, source_target_pairs={{0,1},{1,2},{2,3},{3,0},{4,5},{5,6},{6,7},{7,4},{8,9},{9,10},{10,1... | collective-permute-start | bytes 983048 | tf_op jit(solution)/shard_map/while/body/eval_jaxpr/ppermute | solution.py:10
  53.8 11.1 %collective-permute-done.2 = bf16[128,10,128]{2,0,1:T(8,128)(2,1)} collective-permute-done((bf16[128,10,128]{2,0,1:T(8,128)(2,1)}, bf16[128,10,128]{2,0,1:T(8,128)(2,1)}, u32[]{:S(2)}, u32[]{:S(2)}) %collective-permute-start.2) | collective-permute-done | bytes 327712 | tf_op jit(solution)/shard_map/while/body/eval_jaxpr/ppermute | solution.py:10
  64.8 1.9 convert_element_type.94
  69.3 1.4 fusion.47
  70.7 2.1 fusion.48
  72.8 2.5 %collective-permute-start.2 = (bf16[128,10,128]{2,0,1:T(8,128)(2,1)}, bf16[128,10,128]{2,0,1:T(8,128)(2,1)}, u32[]{:S(2)}, u32[]{:S(2)}) collective-permute-start(bf16[128,10,128]{2,0,1:T(8,128)(2,1)} %fusion.48), channel_id=1, source_target_pairs={{0,1},{1,2},{2,3},{3,0},{4,5},{5,6},{6,7},{7,4},{8,9},{9,10},{10,1... | collective-permute-start | bytes 983048 | tf_op jit(solution)/shard_map/while/body/eval_jaxpr/ppermute | solution.py:10
  75.2 2.3 fusion.49
  78.0 8.8 %collective-permute-done.2 = bf16[128,10,128]{2,0,1:T(8,128)(2,1)} collective-permute-done((bf16[128,10,128]{2,0,1:T(8,128)(2,1)}, bf16[128,10,128]{2,0,1:T(8,128)(2,1)}, u32[]{:S(2)}, u32[]{:S(2)}) %collective-permute-start.2) | collective-permute-done | bytes 327712 | tf_op jit(solution)/shard_map/while/body/eval_jaxpr/ppermute | solution.py:10
  86.8 1.9 convert_element_type.94
  91.3 1.4 fusion.47
  92.6 2.1 fusion.48
  94.7 2.5 %collective-permute-start.2 = (bf16[128,10,128]{2,0,1:T(8,128)(2,1)}, bf16[128,10,128]{2,0,1:T(8,128)(2,1)}, u32[]{:S(2)}, u32[]{:S(2)}) collective-permute-start(bf16[128,10,128]{2,0,1:T(8,128)(2,1)} %fusion.48), channel_id=1, source_target_pairs={{0,1},{1,2},{2,3},{3,0},{4,5},{5,6},{6,7},{7,4},{8,9},{9,10},{10,1... | collective-permute-start | bytes 983048 | tf_op jit(solution)/shard_map/while/body/eval_jaxpr/ppermute | solution.py:10
  97.2 2.3 fusion.49
  99.9 8.8 %collective-permute-done.2 = bf16[128,10,128]{2,0,1:T(8,128)(2,1)} collective-permute-done((bf16[128,10,128]{2,0,1:T(8,128)(2,1)}, bf16[128,10,128]{2,0,1:T(8,128)(2,1)}, u32[]{:S(2)}, u32[]{:S(2)}) %collective-permute-start.2) | collective-permute-done | bytes 327712 | tf_op jit(solution)/shard_map/while/body/eval_jaxpr/ppermute | solution.py:10
  108.7 1.9 convert_element_type.94
  114.5 2.1 fusion.48
  116.6 2.5 %collective-permute-start.2 = (bf16[128,10,128]{2,0,1:T(8,128)(2,1)}, bf16[128,10,128]{2,0,1:T(8,128)(2,1)}, u32[]{:S(2)}, u32[]{:S(2)}) collective-permute-start(bf16[128,10,128]{2,0,1:T(8,128)(2,1)} %fusion.48), channel_id=1, source_target_pairs={{0,1},{1,2},{2,3},{3,0},{4,5},{5,6},{6,7},{7,4},{8,9},{9,10},{10,1... | collective-permute-start | bytes 983048 | tf_op jit(solution)/shard_map/while/body/eval_jaxpr/ppermute | solution.py:10
  119.1 2.3 fusion.49
  121.8 7.1 %collective-permute-done.2 = bf16[128,10,128]{2,0,1:T(8,128)(2,1)} collective-permute-done((bf16[128,10,128]{2,0,1:T(8,128)(2,1)}, bf16[128,10,128]{2,0,1:T(8,128)(2,1)}, u32[]{:S(2)}, u32[]{:S(2)}) %collective-permute-start.2) | collective-permute-done | bytes 327712 | tf_op jit(solution)/shard_map/while/body/eval_jaxpr/ppermute | solution.py:10
  128.9 1.9 convert_element_type.94
  131.0 4.6 %fusion.9 = bf16[2560,1280]{0,1:T(8,128)(2,1)} fusion(bf16[128,1280]{0,1:T(8,128)(2,1)S(1)} %bitcast.82, bf16[1,128,2560]{2,1,0:T(8,128)(2,1)S(1)} %copy-done), kind=kOutput, calls=%fused_computation.17 | convolution fusion | flops 842137600 | bytes 7536640 | tf_op jit(solution)/shard_map/tf,tw->fw/dot_general | solution.py:78
  135.6 9.5 %copy.72 = bf16[2560,1280]{1,0:T(8,128)(2,1)} copy(bf16[2560,1280]{0,1:T(8,128)(2,1)} %fusion.9) | data formatting | bytes 13107200
  145.2 61.4 %reduce-scatter.7.cloned.1.call-done = bf16[320,1280]{1,0:T(8,128)(2,1)} async-done(((bf16[2560,1280]{1,0:T(8,128)(2,1)}), bf16[320,1280]{1,0:T(8,128)(2,1)}) %reduce-scatter.7.cloned.1.call-update) | async-done | bytes 819216
  206.5 2.2 copy.73
  212.1 23.1 %reduce-scatter.5.cloned.1.call-done = bf16[320,320]{0,1:T(8,128)(2,1)} async-done(((bf16[320,1280]{0,1:T(8,128)(2,1)}), bf16[320,320]{0,1:T(8,128)(2,1)}) %reduce-scatter.5.cloned.1.call-update) | async-done | bytes 204816 | tf_op jit(solution)/shard_map/reduce_scatter | solution.py:85
  235.2 1.9 copy.65
  (68 shorter events, 24.7 us)
Async XLA Ops:
  7.2 123.9 %copy-start = (bf16[1,128,2560]{2,1,0:T(8,128)(2,1)S(1)}, bf16[1,128,2560]{2,1,0:T(8,128)(2,1)}, u32[]{:S(2)}) copy-start(bf16[1,128,2560]{2,1,0:T(8,128)(2,1)} %param.9) | copy-start | bytes 1966084
  7.2 199.4 %reduce-scatter.7.cloned.1.call-start = ((), (), s32[]{:S(2)}) async-start(), calls=%async_computation.3 | async-start | bytes 7372800
  44.8 21.9 %collective-permute-start = (bf16[1,128,1280]{1,2,0:T(8,128)(2,1)S(1)}, bf16[1,128,1280]{1,2,0:T(8,128)(2,1)}, u32[]{:S(2)}, u32[]{:S(2)}) collective-permute-start(bf16[1,128,1280]{1,2,0:T(8,128)(2,1)S(1)} %copy.81), channel_id=1, source_target_pairs={{0,1},{1,2},{2,3},{3,0},{4,5},{5,6},{6,7},{7,4},{8,9},{9,10},{10,1... | collective-permute-start | bytes 983048 | tf_op jit(solution)/shard_map/while/body/eval_jaxpr/ppermute | solution.py:10
  46.4 20.4 %collective-permute-start.1 = (bf16[1,128,1280]{1,2,0:T(8,128)(2,1)S(1)}, bf16[1,128,1280]{1,2,0:T(8,128)(2,1)S(1)}, u32[]{:S(2)}, u32[]{:S(2)}) collective-permute-start(bf16[1,128,1280]{1,2,0:T(8,128)(2,1)S(1)} %copy.82), channel_id=1, source_target_pairs={{0,1},{1,2},{2,3},{3,0},{4,5},{5,6},{6,7},{7,4},{8,9},{9,10},{10,1... | collective-permute-start | bytes 983048 | tf_op jit(solution)/shard_map/while/body/eval_jaxpr/ppermute | solution.py:10
  49.2 15.6 %collective-permute-start.2 = (bf16[128,10,128]{2,0,1:T(8,128)(2,1)}, bf16[128,10,128]{2,0,1:T(8,128)(2,1)}, u32[]{:S(2)}, u32[]{:S(2)}) collective-permute-start(bf16[128,10,128]{2,0,1:T(8,128)(2,1)} %fusion.48), channel_id=1, source_target_pairs={{0,1},{1,2},{2,3},{3,0},{4,5},{5,6},{6,7},{7,4},{8,9},{9,10},{10,1... | collective-permute-start | bytes 983048 | tf_op jit(solution)/shard_map/while/body/eval_jaxpr/ppermute | solution.py:10
  67.7 20.9 %collective-permute-start = (bf16[1,128,1280]{1,2,0:T(8,128)(2,1)S(1)}, bf16[1,128,1280]{1,2,0:T(8,128)(2,1)}, u32[]{:S(2)}, u32[]{:S(2)}) collective-permute-start(bf16[1,128,1280]{1,2,0:T(8,128)(2,1)S(1)} %copy.81), channel_id=1, source_target_pairs={{0,1},{1,2},{2,3},{3,0},{4,5},{5,6},{6,7},{7,4},{8,9},{9,10},{10,1... | collective-permute-start | bytes 983048 | tf_op jit(solution)/shard_map/while/body/eval_jaxpr/ppermute | solution.py:10
  67.8 20.9 %collective-permute-start.1 = (bf16[1,128,1280]{1,2,0:T(8,128)(2,1)S(1)}, bf16[1,128,1280]{1,2,0:T(8,128)(2,1)S(1)}, u32[]{:S(2)}, u32[]{:S(2)}) collective-permute-start(bf16[1,128,1280]{1,2,0:T(8,128)(2,1)S(1)} %copy.82), channel_id=1, source_target_pairs={{0,1},{1,2},{2,3},{3,0},{4,5},{5,6},{6,7},{7,4},{8,9},{9,10},{10,1... | collective-permute-start | bytes 983048 | tf_op jit(solution)/shard_map/while/body/eval_jaxpr/ppermute | solution.py:10
  72.8 14.0 %collective-permute-start.2 = (bf16[128,10,128]{2,0,1:T(8,128)(2,1)}, bf16[128,10,128]{2,0,1:T(8,128)(2,1)}, u32[]{:S(2)}, u32[]{:S(2)}) collective-permute-start(bf16[128,10,128]{2,0,1:T(8,128)(2,1)} %fusion.48), channel_id=1, source_target_pairs={{0,1},{1,2},{2,3},{3,0},{4,5},{5,6},{6,7},{7,4},{8,9},{9,10},{10,1... | collective-permute-start | bytes 983048 | tf_op jit(solution)/shard_map/while/body/eval_jaxpr/ppermute | solution.py:10
  89.7 20.9 %collective-permute-start = (bf16[1,128,1280]{1,2,0:T(8,128)(2,1)S(1)}, bf16[1,128,1280]{1,2,0:T(8,128)(2,1)}, u32[]{:S(2)}, u32[]{:S(2)}) collective-permute-start(bf16[1,128,1280]{1,2,0:T(8,128)(2,1)S(1)} %copy.81), channel_id=1, source_target_pairs={{0,1},{1,2},{2,3},{3,0},{4,5},{5,6},{6,7},{7,4},{8,9},{9,10},{10,1... | collective-permute-start | bytes 983048 | tf_op jit(solution)/shard_map/while/body/eval_jaxpr/ppermute | solution.py:10
  89.7 20.9 %collective-permute-start.1 = (bf16[1,128,1280]{1,2,0:T(8,128)(2,1)S(1)}, bf16[1,128,1280]{1,2,0:T(8,128)(2,1)S(1)}, u32[]{:S(2)}, u32[]{:S(2)}) collective-permute-start(bf16[1,128,1280]{1,2,0:T(8,128)(2,1)S(1)} %copy.82), channel_id=1, source_target_pairs={{0,1},{1,2},{2,3},{3,0},{4,5},{5,6},{6,7},{7,4},{8,9},{9,10},{10,1... | collective-permute-start | bytes 983048 | tf_op jit(solution)/shard_map/while/body/eval_jaxpr/ppermute | solution.py:10
  94.7 14.0 %collective-permute-start.2 = (bf16[128,10,128]{2,0,1:T(8,128)(2,1)}, bf16[128,10,128]{2,0,1:T(8,128)(2,1)}, u32[]{:S(2)}, u32[]{:S(2)}) collective-permute-start(bf16[128,10,128]{2,0,1:T(8,128)(2,1)} %fusion.48), channel_id=1, source_target_pairs={{0,1},{1,2},{2,3},{3,0},{4,5},{5,6},{6,7},{7,4},{8,9},{9,10},{10,1... | collective-permute-start | bytes 983048 | tf_op jit(solution)/shard_map/while/body/eval_jaxpr/ppermute | solution.py:10
  111.6 19.2 %collective-permute-start = (bf16[1,128,1280]{1,2,0:T(8,128)(2,1)S(1)}, bf16[1,128,1280]{1,2,0:T(8,128)(2,1)}, u32[]{:S(2)}, u32[]{:S(2)}) collective-permute-start(bf16[1,128,1280]{1,2,0:T(8,128)(2,1)S(1)} %copy.81), channel_id=1, source_target_pairs={{0,1},{1,2},{2,3},{3,0},{4,5},{5,6},{6,7},{7,4},{8,9},{9,10},{10,1... | collective-permute-start | bytes 983048 | tf_op jit(solution)/shard_map/while/body/eval_jaxpr/ppermute | solution.py:10
  111.6 19.2 %collective-permute-start.1 = (bf16[1,128,1280]{1,2,0:T(8,128)(2,1)S(1)}, bf16[1,128,1280]{1,2,0:T(8,128)(2,1)S(1)}, u32[]{:S(2)}, u32[]{:S(2)}) collective-permute-start(bf16[1,128,1280]{1,2,0:T(8,128)(2,1)S(1)} %copy.82), channel_id=1, source_target_pairs={{0,1},{1,2},{2,3},{3,0},{4,5},{5,6},{6,7},{7,4},{8,9},{9,10},{10,1... | collective-permute-start | bytes 983048 | tf_op jit(solution)/shard_map/while/body/eval_jaxpr/ppermute | solution.py:10
  116.6 12.3 %collective-permute-start.2 = (bf16[128,10,128]{2,0,1:T(8,128)(2,1)}, bf16[128,10,128]{2,0,1:T(8,128)(2,1)}, u32[]{:S(2)}, u32[]{:S(2)}) collective-permute-start(bf16[128,10,128]{2,0,1:T(8,128)(2,1)} %fusion.48), channel_id=1, source_target_pairs={{0,1},{1,2},{2,3},{3,0},{4,5},{5,6},{6,7},{7,4},{8,9},{9,10},{10,1... | collective-permute-start | bytes 983048 | tf_op jit(solution)/shard_map/while/body/eval_jaxpr/ppermute | solution.py:10
  145.1 63.7 %copy-start.2 = (f32[128,10,128]{2,0,1:T(8,128)S(1)}, f32[128,10,128]{2,0,1:T(8,128)}, u32[]{:S(2)}) copy-start(f32[128,10,128]{2,0,1:T(8,128)} %get-tuple-element.271) | copy-start | bytes 1966084
  145.1 65.8 %copy-start.1 = (f32[128,10,128]{2,0,1:T(8,128)S(1)}, f32[128,10,128]{2,0,1:T(8,128)}, u32[]{:S(2)}) copy-start(f32[128,10,128]{2,0,1:T(8,128)} %get-tuple-element.272) | copy-start | bytes 1966084
  145.1 90.1 %reduce-scatter.5.cloned.1.call-start = ((), (), s32[]{:S(2)}) async-start(), calls=%async_computation.2 | async-start | bytes 1228800 | tf_op jit(solution)/shard_map/reduce_scatter | solution.py:85
Sparse Core Ops, SparseCore 0:
  145.2 61.2 reduce-scatter.6
  208.9 26.2 reduce-scatter.4
where the time goes:
time: 245 us; the launch traced here: 244 us
  waiting for transfers between devices  120 us (49%)
  local copies, waits for them, and re-layouts  29.4 us (12%)
  matrix products  28.4 us (12%)
  blocking collectives  28 us (11%)
  starting transfers between devices  15.6 us (6%)
  between operations  14.2 us (6%)
  other arithmetic  7.92 us (3%)
    unnamed x3, waiting for transfers between devices  61.4 us
    ppermute x12, waiting for transfers between devices, passed_along(): return lax.ppermute(value, axis, pairs)  35.8 us
    unnamed x20, local copies, waits for them, and re-layouts  24.8 us
    reduce_scatter x1, waiting for transfers between devices, on_device(): lax.psum_scatter(row_sums, 'cp', scatter_dimension=1, tiled=True)  23.1 us
    ppermute x12, starting transfers between devices, passed_along(): return lax.ppermute(value, axis, pairs)  15.5 us
    all_gather x1, blocking collectives, on_device(): lax.all_gather(log_sums, 'cp', axis=1, tiled=True)  14.8 us
    all_gather x1, blocking collectives, on_device(): lax.all_gather(row_delta, 'cp', axis=1, tiled=True)  13.1 us
    dot_general x4, matrix products, cycle_step(): jnp.einsum('hqk,qhd->khd', grad_score, query_heads, preferred_element_typ...  8.16 us
  transfers between devices with their start and end apart: 14, of which 6 were waited for; matrix products, arithmetic and copies ran while one was open for 14% of the time, Pallas kernels for 0%

commit v1 on v0

v1 whole, which is shorter than its diff:
```python
import functools
import math

import jax
import jax.numpy as jnp
from jax import lax
from jax.experimental import pallas as pl
from jax.experimental.pallas import tpu as pltpu
from jax.sharding import PartitionSpec as P

F32 = jnp.float32
BF16 = jnp.bfloat16
PARTS = 6


def three_parts(row):
    high = row.astype(BF16).astype(F32)
    rest = row - high
    mid = rest.astype(BF16).astype(F32)
    return high, mid, rest - mid


def extra_rows(count):
    return -(-count * PARTS // 16) * 16


def head_groups(per_pos, groups):
    if groups != 2 or per_pos < 3:
        return [list(range(per_pos))]
    first = [h for h in range(per_pos) if h % 2 == 0 or per_pos % 2 == 0 and h in (0, per_pos - 1)]
    first = sorted(set(first) | {per_pos - 1 - h for h in first})
    second = [h for h in range(per_pos) if h not in first]
    return [first, second] if second else [first]


def column_runs(chunks, per_pos, groups, head_size):
    width = per_pos * head_size // groups
    runs = []
    for owner in range(groups):
        found = []
        for index, heads in enumerate(chunks):
            piece = len(heads) * head_size // groups
            unit = math.gcd(piece, head_size)
            for start in range(0, piece, unit):
                at = owner * piece + start
                column = heads[at // head_size] * head_size + at % head_size
                found.append((column - owner * width, index, start, unit))
        found.sort()
        place = 0
        for column, _, _, unit in found:
            assert column == place
            place += unit
        assert place == width
        runs.append([(index, start, unit) for _, index, start, unit in found])
    return runs


def pack_kernel(dims, heads, q_ref, k_ref, v_ref, o_ref, g_ref, norm_ref, *outs):
    members, groups, per_pos, tokens, size = dims
    pos = lax.rem(lax.axis_index("cp"), members)
    extra = extra_rows(len(heads))
    ones = jnp.ones((8, size), BF16)
    row_id = lax.broadcasted_iota(jnp.int32, (extra, tokens), 0)
    for b in range(members):
        owner = lax.rem(pos + b, members)
        full = outs[b]
        side = jnp.zeros((extra, tokens), F32)
        for i, head in enumerate(heads):
            number = owner * per_pos + head
            lanes = pl.ds(pl.multiple_of(number * size, size), size)
            grad = g_ref[:, lanes]
            product = grad.astype(F32) * o_ref[:, lanes].astype(F32)
            high = product.astype(BF16)
            low = (product - high.astype(F32)).astype(BF16)
            contract = (((1,), (1,)), ((), ()))
            delta = lax.dot_general(ones, high, contract, preferred_element_type=F32)
            delta += lax.dot_general(ones, low, contract, preferred_element_type=F32)
            norm = norm_ref[pl.ds(number, 1), :]
            values = three_parts(norm) + three_parts(delta[0:1, :])
            for part, value in enumerate(values):
                side = jnp.where(row_id == i * PARTS + part, value, side)
            at = 2 * i * tokens
            query = q_ref[:, lanes]
            base = 2 * len(heads) * tokens + extra + at
            full[at : at + tokens, :] = query
            full[at + tokens : at + 2 * tokens, :] = grad
            full[base : base + tokens, :] = k_ref[:, lanes]
            full[base + tokens : base + 2 * tokens, :] = v_ref[:, lanes]
            if groups > 1:
                outs[members + b][at : at + tokens, :] = query
                outs[members + b][at + tokens : at + 2 * tokens, :] = grad
        at = 2 * len(heads) * tokens
        side = side.astype(BF16)
        full[at : at + extra, :] = side
        if groups > 1:
            outs[members + b][at : at + extra, :] = side


def attn_kernel(dims, count, *refs):
    members, groups, _, tokens, size = dims
    sources = members * groups
    blocks = refs[:sources]
    grad_value, returns = refs[sources], refs[sources + 1 :]
    scale = size ** (-0.5)
    extra = extra_rows(count)
    side_at = 2 * count * tokens
    sides = [block[side_at : side_at + extra, :].astype(F32) for block in blocks]
    rows_rows = (((1,), (1,)), ((), ()))

    def side_row(first):
        return jnp.concatenate(
            [s[first : first + 1] + s[first + 1 : first + 2] + s[first + 2 : first + 3] for s in sides],
            axis=1,
        )

    for i in range(count):
        at = 2 * i * tokens
        kv_at = side_at + extra + at
        lanes = slice(i * size, (i + 1) * size)
        keys = jnp.concatenate([blocks[b][kv_at : kv_at + tokens, :] for b in range(members)], axis=0)
        values = jnp.concatenate(
            [blocks[b][kv_at + tokens : kv_at + 2 * tokens, :] for b in range(members)], axis=0
        )
        queries = jnp.concatenate([block[at : at + tokens, :] for block in blocks], axis=0)
        grads = jnp.concatenate([block[at + tokens : at + 2 * tokens, :] for block in blocks], axis=0)
        scores = lax.dot_general(keys, queries, rows_rows, preferred_element_type=F32)
        prob = jnp.exp(scores * scale - side_row(i * PARTS))
        grad_v = jnp.dot(prob.astype(BF16), grads, preferred_element_type=F32).astype(BF16)
        grad_value[:, lanes] = grad_v
        grad_prob = lax.dot_general(values, grads, rows_rows, preferred_element_type=F32)
        grad_score = (prob * (grad_prob - side_row(i * PARTS + 3))).astype(BF16)
        grad_k = (scale * jnp.dot(grad_score, queries, preferred_element_type=F32)).astype(BF16)
        grad_q = lax.dot_general(
            grad_score, keys, (((0,), (0,)), ((), ())), preferred_element_type=F32
        )
        grad_q = (scale * grad_q).astype(BF16)
        for source in range(sources):
            rows = slice(source * tokens, (source + 1) * tokens)
            returns[source][:, lanes] = grad_q[rows]
            if source < members:
                second = slice((count + i) * size, (count + i + 1) * size)
                third = slice((2 * count + i) * size, (2 * count + i + 1) * size)
                returns[source][:, second] = grad_k[rows]
                returns[source][:, third] = grad_v[rows]


def finish_kernel(dims, chunks, *refs):
    members, groups, per_pos, _, size = dims
    sources = members * groups
    pos = lax.rem(lax.axis_index("cp"), members)
    returned = refs[: sources * len(chunks)]
    d_query, d_key, d_value = refs[sources * len(chunks) :]
    for b in range(members):
        owner = lax.rem(pos + b, members)
        for index, heads in enumerate(chunks):
            mine = returned[index * sources : (index + 1) * sources]
            for i, head in enumerate(heads):
                lanes = pl.ds(pl.multiple_of((owner * per_pos + head) * size, size), size)
                part = slice(i * size, (i + 1) * size)
                total = mine[b][:, part].astype(F32)
                for a in range(1, groups):
                    total += mine[a * members + b][:, part].astype(F32)
                d_query[:, lanes] = total.astype(BF16)
                count = len(heads)
                d_key[:, lanes] = mine[b][:, (count + i) * size : (count + i + 1) * size]
                d_value[:, lanes] = mine[b][:, (2 * count + i) * size : (2 * count + i + 1) * size]


def weight_kernel(chips, cores, *refs):
    features, grads = refs[:chips], refs[chips : 2 * chips]
    outs, total = refs[2 * chips : 2 * chips + cores], refs[-1]
    sums = None
    for x, g in zip(features, grads):
        term = lax.dot_general(x[...], g[...], (((0,), (0,)), ((), ())), preferred_element_type=F32)
        sums = term if sums is None else sums + term
    total[...] = sums
    core = lax.rem(lax.axis_index("fsdp"), cores)
    rows = outs[0].shape[0]
    for c, out in enumerate(outs):
        at = pl.multiple_of(lax.rem(core + c, cores) * rows, 16)
        out[...] = total[pl.ds(at, rows), :].astype(out.dtype)


def call(kernel, shapes, args, flops=0, exps=0, scratch=()):
    moved = sum(a.size * a.dtype.itemsize for a in args) + sum(
        math.prod(s.shape) * s.dtype.itemsize for s in shapes
    )
    return pl.pallas_call(
        kernel,
        out_shape=tuple(shapes),
        in_specs=[pl.BlockSpec(memory_space=pltpu.VMEM)] * len(args),
        out_specs=tuple(pl.BlockSpec(memory_space=pltpu.VMEM) for _ in shapes),
        scratch_shapes=scratch,
        cost_estimate=pl.CostEstimate(flops=flops, bytes_accessed=moved, transcendentals=exps),
    )(*args)


def on_device(features, query_rows, key_rows, value_rows, attn_output, grad_output, log_sums):
    tokens, width = query_rows.shape[1:]
    total_heads = log_sums.shape[2]
    size = width // total_heads
    spread, fleet = lax.axis_size("cp"), lax.axis_size("fsdp")
    members = math.gcd(spread, total_heads)
    groups = spread // members
    per_pos = total_heads // members
    cores = 2 if fleet % 2 == 0 else 1
    chips = fleet // cores
    dims = (members, groups, per_pos, tokens, size)
    chunks = head_groups(per_pos, groups)
    owned = column_runs(chunks, per_pos, groups, size)
    place = lax.axis_index("cp")
    group, pos = place // members, place % members
    unit = lax.axis_index("fsdp")

    def peer(index, a, b):
        return (index // members + a) % groups * members + (index % members + b) % members

    def send(value, a, b):
        return lax.ppermute(value, "cp", [(i, peer(i, a, b)) for i in range(spread)])

    def send_back(value, a, b):
        return lax.ppermute(value, "cp", [(peer(i, a, b), i) for i in range(spread)])

    def other_chip(chip, k):
        return chip ^ k if chips & (chips - 1) == 0 else (chip + k) % chips

    def to_chip(value, k):
        pairs = [(i, other_chip(i // cores, k) * cores + i % cores) for i in range(fleet)]
        return lax.ppermute(value, "fsdp", pairs)

    shifts = [(a, b) for a in range(groups) for b in range(members)]
    flat = [v[0] for v in (query_rows, key_rows, value_rows, attn_output, grad_output)]
    norms = log_sums[0].T

    arrived = []
    for heads in chunks:
        short = 2 * len(heads) * tokens + extra_rows(len(heads))
        long = short + 2 * len(heads) * tokens
        shapes = [jax.ShapeDtypeStruct((long, size), BF16)] * members
        if groups > 1:
            shapes += [jax.ShapeDtypeStruct((short, size), BF16)] * members
        packed = call(functools.partial(pack_kernel, dims, heads), shapes, (*flat, norms))
        blocks = [packed[0]]
        for a, b in shifts[1:]:
            blocks.append(send(packed[b if a == 0 else members + b], a, b))
        arrived.append(blocks)

    pieces = [features[0]] + [send(features, 0, b)[0] for b in range(1, members)]
    chip_rows = features.shape[2] // chips
    columns = []
    for k in range(chips):
        start = other_chip(unit // cores, k) * chip_rows
        block = jnp.concatenate(
            [lax.dynamic_slice_in_dim(p, start, chip_rows, 1) for p in pieces], axis=0
        )
        columns.append(block if k == 0 else to_chip(block, k))

    returned, weight_parts = [], []
    for heads, blocks in zip(chunks, arrived):
        count = len(heads)
        shapes = [jax.ShapeDtypeStruct((members * tokens, count * size), BF16)]
        for a, b in shifts:
            shapes.append(jax.ShapeDtypeStruct((tokens, (3 if a == 0 else 1) * count * size), BF16))
        area = members * tokens * spread * tokens * count
        grad_value, *back = call(
            functools.partial(attn_kernel, dims, count), shapes, blocks, 10 * area * size, area
        )
        gathered = [grad_value] + [to_chip(grad_value, k) for k in range(1, chips)]
        returned.append(back[:1] + [send_back(r, a, b) for r, (a, b) in zip(back[1:], shifts[1:])])

        rows = chip_rows // cores
        shapes = [jax.ShapeDtypeStruct((rows, count * size), F32)]
        shapes += [jax.ShapeDtypeStruct((rows, count * size), BF16)] * (cores - 1)
        own, *others = call(
            functools.partial(weight_kernel, chips, cores),
            shapes,
            (*columns, *gathered),
            2 * chip_rows * count * size * chips * members * tokens,
            scratch=[pltpu.VMEM((chip_rows, count * size), F32)],
        )
        for c, other in enumerate(others, 1):
            pairs = [(i, i // cores * cores + (i + c) % cores) for i in range(fleet)]
            own = own + lax.ppermute(other, "fsdp", pairs).astype(F32)
        piece = count * size // groups
        total = None
        for r in range(groups):
            block = lax.dynamic_slice_in_dim(own, (group + r) % groups * piece, piece, 1).astype(BF16)
            pairs = [
                (g * members + p, p * groups + (g + r) % groups)
                for g in range(groups)
                for p in range(members)
            ]
            block = lax.ppermute(block, "cp", pairs).astype(F32)
            total = block if total is None else total + block
        weight_parts.append(total)

    shapes = [jax.ShapeDtypeStruct((tokens, width), BF16)] * 3
    d_query, d_key, d_value = call(
        functools.partial(finish_kernel, dims, chunks), shapes, [r for back in returned for r in back]
    )

    def assembled(owner):
        return jnp.concatenate(
            [weight_parts[i][:, s : s + n] for i, s, n in owned[owner]], axis=1
        )

    weight = assembled(0)
    for owner in range(1, groups):
        if owned[owner] != owned[0]:
            weight = jnp.where(place % groups == owner, assembled(owner), weight)
    return (d_query[None], d_key[None], d_value[None], weight)


def solution(mesh):
    tokens = P("fsdp", "cp", None)
    return jax.shard_map(
        on_device,
        mesh=mesh,
        in_specs=(tokens,) * 7,
        out_specs=(tokens, tokens, tokens, P("fsdp", "cp")),
        check_vma=False,
    )
```

time: 245 us -> 112 us (0.46)
  waiting for transfers between devices: 120 us -> 42.9 us
  matrix products: 28.4 us -> 0 us
  blocking collectives: 28 us -> 0 us
  starting transfers between devices: 15.6 us -> 39.8 us
  local copies, waits for them, and re-layouts: 29.4 us -> 5.99 us
  Pallas kernels: 0 us -> 20.4 us
  between operations: 14.2 us -> 0.88 us
  other arithmetic: 7.92 us -> 2 us
    unnamed x3 -> x0, waiting for transfers between devices: 61.4 us -> none
    dot_general x21 -> x0, matrix products: 28.4 us -> none  [the longest x4 8.16 us: cycle_step(): jnp.einsum('hqk,qhd->khd', grad_score, query_heads, preferred_element_typ...]
    all_gather x2 -> x0, blocking collectives: 28 us -> none  [the longest x1 14.8 us: on_device(): lax.all_gather(log_sums, 'cp', axis=1, tiled=True)]
    ppermute x12 -> x28, starting transfers between devices: 15.5 us -> 39.8 us  [the longest x9 12.5 us: to_chip(): return lax.ppermute(value, 'fsdp', pairs)]
    reduce_scatter x1 -> x0, waiting for transfers between devices: 23.1 us -> none  [on_device(): lax.psum_scatter(row_sums, 'cp', scatter_dimension=1, tiled=True)]
    pallas_call x0 -> x7, Pallas kernels: none -> 20.4 us  [call(): pl.pallas_call(kernel, out_shape=tuple(shapes), in_specs=[pl.BlockSpec(me...]
    unnamed x20 -> x51, local copies, waits for them, and re-layouts: 24.8 us -> 5.56 us
    convert_element_type x6 -> x0, other arithmetic: 7.8 us -> none  [the longest x4 7.65 us: cycle_step(): passed_along(query_run.astype(jnp.bfloat16), 'cp', 1)]
  transfers between devices with their start and end apart: 14 -> 28, of which waited for: 6 -> 11; matrix products, arithmetic and copies ran while one was open for 14% -> 2% of each run, Pallas kernels for 0% -> 18%
where the time goes in v1:
time: 112 us
  waiting for transfers between devices  42.9 us (38%)
  starting transfers between devices  39.8 us (36%)
  Pallas kernels  20.4 us (18%)
  local copies, waits for them, and re-layouts  5.99 us (5%)
  other arithmetic  2 us (2%)
    pallas_call x7, Pallas kernels, call(): pl.pallas_call(kernel, out_shape=tuple(shapes), in_specs=[pl.BlockSpec(me...  20.4 us
    ppermute x7, waiting for transfers between devices, send(): lax.ppermute(value, 'cp', [(i, peer(i, a, b)) for i in range(spread)])  20.1 us
    ppermute x9, starting transfers between devices, to_chip(): return lax.ppermute(value, 'fsdp', pairs)  12.5 us
    ppermute x7, starting transfers between devices, send(): lax.ppermute(value, 'cp', [(i, peer(i, a, b)) for i in range(spread)])  12.4 us
    ppermute x6, starting transfers between devices, send_back(): lax.ppermute(value, 'cp', [(peer(i, a, b), i) for i in range(spread)])  8.82 us
    ppermute x6, waiting for transfers between devices, send_back(): lax.ppermute(value, 'cp', [(peer(i, a, b), i) for i in range(spread)])  8.25 us
    ppermute x9, waiting for transfers between devices, to_chip(): return lax.ppermute(value, 'fsdp', pairs)  7.66 us
    ppermute x4, waiting for transfers between devices, on_device(): block = lax.ppermute(block, 'cp', pairs).astype(F32)  6.34 us
  transfers between devices with their start and end apart: 28, of which 11 were waited for; matrix products, arithmetic and copies ran while one was open for 2% of the time, Pallas kernels for 18%

profile of v1, /device:TPU:0, one launch (start us, length us, event | category | flops | bytes accessed | tf_op | source)
XLA Modules:
  0.0 112.0 jit_solution(13470991508532416774)
XLA Ops:
  0.6 3.1 %collective-permute-start.12 = (bf16[1,128,2560]{2,1,0:T(8,128)(2,1)}, bf16[1,128,2560]{2,1,0:T(8,128)(2,1)S(1)}, u32[]{:S(2)}, u32[]{:S(2)}) collective-permute-start(bf16[1,128,2560]{2,1,0:T(8,128)(2,1)} %param.7), channel_id=1, source_target_pairs={{0,1},{1,0},{2,3},{3,2},{4,5},{5,4},{6,7},{7,6},{8,9},{9,8},{10,11... | collective-permute-start | bytes 1966088 | tf_op jit(solution)/shard_map/ppermute | solution.py:219
  5.0 2.5 %shard_map.104 = (bf16[1040,128]{1,0:T(8,128)(2,1)}, bf16[1040,128]{1,0:T(8,128)(2,1)}, bf16[528,128]{1,0:T(8,128)(2,1)}, bf16[528,128]{1,0:T(8,128)(2,1)}) custom-call(bf16[128,1280]{1,0:T(8,128)(2,1)} %bitcast.29, bf16[128,1280]{1,0:T(8,128)(2,1)} %bitcast.31, bf16[128,1280]{1,0:T(8,128)(2,1)} %bitcast.33, bf16[128,1280]{1,0:T(8,128)(2,1)} %bitcast.35, ...), custom_call_target="tpu_custom_call" | custom-call | bytes 2446336 | tf_op jit(solution)/shard_map/pallas_call | solution.py:188
  7.6 3.0 %collective-permute-start.7 = (bf16[528,128]{1,0:T(8,128)(2,1)}, bf16[528,128]{1,0:T(8,128)(2,1)S(1)}, u32[]{:S(2)}, u32[]{:S(2)}) collective-permute-start(bf16[528,128]{1,0:T(8,128)(2,1)} %get-tuple-element.39), channel_id=1, source_target_pairs={{0,2},{1,3},{2,0},{3,1},{4,6},{5,7},{6,4},{7,5},{8,10},{9,11},{10,... | collective-permute-start | bytes 405512 | tf_op jit(solution)/shard_map/ppermute | solution.py:219
  10.6 1.3 %collective-permute-start.8 = (bf16[528,128]{1,0:T(8,128)(2,1)}, bf16[528,128]{1,0:T(8,128)(2,1)}, u32[]{:S(2)}, u32[]{:S(2)}) collective-permute-start(bf16[528,128]{1,0:T(8,128)(2,1)} %get-tuple-element.40), channel_id=1, source_target_pairs={{0,3},{1,2},{2,1},{3,0},{4,7},{5,6},{6,5},{7,4},{8,11},{9,10},{10,... | collective-permute-start | bytes 405512 | tf_op jit(solution)/shard_map/ppermute | solution.py:219
  11.9 2.7 %shard_map.102 = (bf16[1568,128]{1,0:T(8,128)(2,1)}, bf16[1568,128]{1,0:T(8,128)(2,1)}, bf16[800,128]{1,0:T(8,128)(2,1)}, bf16[800,128]{1,0:T(8,128)(2,1)}) custom-call(bf16[128,1280]{1,0:T(8,128)(2,1)} %bitcast.30, bf16[128,1280]{1,0:T(8,128)(2,1)} %bitcast.32, bf16[128,1280]{1,0:T(8,128)(2,1)} %bitcast.34, bf16[128,1280]{1,0:T(8,128)(2,1)} %bitcast.36, ...), custom_call_target="tpu_custom_call" | custom-call | bytes 2855936 | tf_op jit(solution)/shard_map/pallas_call | solution.py:188
  15.0 12.8 %collective-permute-done.7.refs_2_ = bf16[528,128]{1,0:T(8,128)(2,1)S(1)} collective-permute-done((bf16[528,128]{1,0:T(8,128)(2,1)}, bf16[528,128]{1,0:T(8,128)(2,1)S(1)}, u32[]{:S(2)}, u32[]{:S(2)}) %collective-permute-start.7) | collective-permute-done | bytes 135200 | tf_op jit(solution)/shard_map/ppermute | solution.py:219
  28.4 3.3 %collective-permute-start.1 = (bf16[800,128]{1,0:T(8,128)(2,1)S(1)}, bf16[800,128]{1,0:T(8,128)(2,1)S(1)}, u32[]{:S(2)}, u32[]{:S(2)}) collective-permute-start(bf16[800,128]{1,0:T(8,128)(2,1)S(1)} %copy-done.20), channel_id=1, source_target_pairs={{0,2},{1,3},{2,0},{3,1},{4,6},{5,7},{6,4},{7,5},{8,10},{9,11},{10,... | collective-permute-start | bytes 614408 | tf_op jit(solution)/shard_map/ppermute | solution.py:219
  31.7 1.9 %collective-permute-done.8.refs_3_ = bf16[528,128]{1,0:T(8,128)(2,1)} collective-permute-done((bf16[528,128]{1,0:T(8,128)(2,1)}, bf16[528,128]{1,0:T(8,128)(2,1)}, u32[]{:S(2)}, u32[]{:S(2)}) %collective-permute-start.8) | collective-permute-done | bytes 135200 | tf_op jit(solution)/shard_map/ppermute | solution.py:219
  35.7 2.9 %shard_map.105 = (bf16[256,256]{1,0:T(8,128)(2,1)}, bf16[128,768]{1,0:T(8,128)(2,1)}, bf16[128,768]{1,0:T(8,128)(2,1)}, bf16[128,256]{1,0:T(8,128)(2,1)}, bf16[128,256]{1,0:T(8,128)(2,1)}) custom-call(bf16[1040,128]{1,0:T(8,128)(2,1)} %get-tuple-element.37.refs_0_, bf16[1040,128]{1,0:T(8,128)(2,1)} %copy-done.18, bf16[528,128]{1,0:T(8,128)(2,1)} %copy-done.22, ...), custom_call_target="tpu_custom_call" | custom-call | flops 335544320 | bytes 1458176 | tf_op jit(solution)/shard_map/pallas_call | solution.py:188
  38.6 1.5 %collective-permute-start.22 = (bf16[256,256]{1,0:T(8,128)(2,1)}, bf16[256,256]{1,0:T(8,128)(2,1)S(1)}, u32[]{:S(2)}, u32[]{:S(2)}) collective-permute-start(bf16[256,256]{1,0:T(8,128)(2,1)} %get-tuple-element.51.refs_4_), channel_id=1, source_target_pairs={{0,8},{4,12},{8,0},{12,4},{16,24},{20,28},{24,16},{28,20},{1,9},{5... | collective-permute-start | bytes 393224 | tf_op jit(solution)/shard_map/ppermute | solution.py:229
  40.1 1.5 %collective-permute-start.23 = (bf16[256,256]{1,0:T(8,128)(2,1)}, bf16[256,256]{1,0:T(8,128)(2,1)S(1)}, u32[]{:S(2)}, u32[]{:S(2)}) collective-permute-start(bf16[256,256]{1,0:T(8,128)(2,1)} %get-tuple-element.51.refs_4_), channel_id=1, source_target_pairs={{0,16},{4,20},{8,24},{12,28},{16,0},{20,4},{24,8},{28,12},{1,17},{... | collective-permute-start | bytes 393224 | tf_op jit(solution)/shard_map/ppermute | solution.py:229
  41.8 1.8 %collective-permute-done.1.refs_2_ = bf16[800,128]{1,0:T(8,128)(2,1)S(1)} collective-permute-done((bf16[800,128]{1,0:T(8,128)(2,1)S(1)}, bf16[800,128]{1,0:T(8,128)(2,1)S(1)}, u32[]{:S(2)}, u32[]{:S(2)}) %collective-permute-start.1) | collective-permute-done | bytes 204832 | tf_op jit(solution)/shard_map/ppermute | solution.py:219
  43.6 3.4 %collective-permute-start.10 = (bf16[128,256]{1,0:T(8,128)(2,1)S(1)}, bf16[128,256]{1,0:T(8,128)(2,1)}, u32[]{:S(2)}, u32[]{:S(2)}) collective-permute-start(bf16[128,256]{1,0:T(8,128)(2,1)S(1)} %copy-done.24), channel_id=1, source_target_pairs={{2,0},{3,1},{0,2},{1,3},{6,4},{7,5},{4,6},{5,7},{10,8},{11,9},{8,1... | collective-permute-start | bytes 196616 | tf_op jit(solution)/shard_map/ppermute | solution.py:222
  47.1 3.6 %collective-permute-done.2.refs_3_ = bf16[800,128]{1,0:T(8,128)(2,1)} collective-permute-done((bf16[800,128]{1,0:T(8,128)(2,1)S(1)}, bf16[800,128]{1,0:T(8,128)(2,1)}, u32[]{:S(2)}, u32[]{:S(2)}) %collective-permute-start.2) | collective-permute-done | bytes 204832 | tf_op jit(solution)/shard_map/ppermute | solution.py:219
  50.7 1.4 %collective-permute-start.11 = (bf16[128,256]{1,0:T(8,128)(2,1)S(1)}, bf16[128,256]{1,0:T(8,128)(2,1)}, u32[]{:S(2)}, u32[]{:S(2)}) collective-permute-start(bf16[128,256]{1,0:T(8,128)(2,1)S(1)} %copy-done.23), channel_id=1, source_target_pairs={{3,0},{2,1},{1,2},{0,3},{7,4},{6,5},{5,6},{4,7},{11,8},{10,9},{9,1... | collective-permute-start | bytes 196616 | tf_op jit(solution)/shard_map/ppermute | solution.py:222
  52.9 1.5 %collective-permute-start.13 = (bf16[256,640]{1,0:T(8,128)(2,1)S(1)}, bf16[256,640]{1,0:T(8,128)(2,1)S(1)}, u32[]{:S(2)}, u32[]{:S(2)}) collective-permute-start(bf16[256,640]{1,0:T(8,128)(2,1)S(1)} %pad_maximum_fusion.1), channel_id=1, source_target_pairs={{0,8},{4,12},{8,0},{12,4},{16,24},{20,28},{24,16},{28,20},{1,9},{5... | collective-permute-start | bytes 983048 | tf_op jit(solution)/shard_map/ppermute | solution.py:229
  54.4 2.4 %collective-permute-done.11.refs_7_ = bf16[128,256]{1,0:T(8,128)(2,1)} collective-permute-done((bf16[128,256]{1,0:T(8,128)(2,1)S(1)}, bf16[128,256]{1,0:T(8,128)(2,1)}, u32[]{:S(2)}, u32[]{:S(2)}) %collective-permute-start.11) | collective-permute-done | bytes 65568 | tf_op jit(solution)/shard_map/ppermute | solution.py:222
  56.8 1.5 %collective-permute-start.14 = (bf16[256,640]{1,0:T(8,128)(2,1)S(1)}, bf16[256,640]{1,0:T(8,128)(2,1)S(1)}, u32[]{:S(2)}, u32[]{:S(2)}) collective-permute-start(bf16[256,640]{1,0:T(8,128)(2,1)S(1)} %pad_maximum_fusion.2), channel_id=1, source_target_pairs={{0,16},{4,20},{8,24},{12,28},{16,0},{20,4},{24,8},{28,12},{1,17},{... | collective-permute-start | bytes 983048 | tf_op jit(solution)/shard_map/ppermute | solution.py:229
  58.4 1.4 %collective-permute-start.15 = (bf16[256,640]{1,0:T(8,128)(2,1)S(1)}, bf16[256,640]{1,0:T(8,128)(2,1)S(1)}, u32[]{:S(2)}, u32[]{:S(2)}) collective-permute-start(bf16[256,640]{1,0:T(8,128)(2,1)S(1)} %pad_maximum_fusion.3), channel_id=1, source_target_pairs={{0,24},{4,28},{8,16},{12,20},{16,8},{20,12},{24,0},{28,4},{1,25},{... | collective-permute-start | bytes 983048 | tf_op jit(solution)/shard_map/ppermute | solution.py:229
  59.8 1.6 %collective-permute-start.24 = (bf16[256,256]{1,0:T(8,128)(2,1)S(1)}, bf16[256,256]{1,0:T(8,128)(2,1)S(1)}, u32[]{:S(2)}, u32[]{:S(2)}) collective-permute-start(bf16[256,256]{1,0:T(8,128)(2,1)S(1)} %copy-done.11), channel_id=1, source_target_pairs={{0,24},{4,28},{8,16},{12,20},{16,8},{20,12},{24,0},{28,4},{1,25},{... | collective-permute-start | bytes 393224 | tf_op jit(solution)/shard_map/ppermute | solution.py:229
  62.1 3.6 %shard_map.103 = (bf16[256,384]{1,0:T(8,128)(2,1)}, bf16[128,1152]{1,0:T(8,128)(2,1)}, bf16[128,1152]{1,0:T(8,128)(2,1)}, bf16[128,384]{1,0:T(8,128)(2,1)}, bf16[128,384]{1,0:T(8,128)(2,1)}) custom-call(bf16[1568,128]{1,0:T(8,128)(2,1)} %get-tuple-element.29.refs_0_, bf16[1568,128]{1,0:T(8,128)(2,1)} %copy-done.17, bf16[800,128]{1,0:T(8,128)(2,1)} %copy-done.21, ...), custom_call_target="tpu_custom_call" | custom-call | flops 503316480 | bytes 2195456 | tf_op jit(solution)/shard_map/pallas_call | solution.py:188
  65.7 7.6 %collective-permute-done.24.refs_7_ = bf16[256,256]{1,0:T(8,128)(2,1)S(1)} collective-permute-done((bf16[256,256]{1,0:T(8,128)(2,1)S(1)}, bf16[256,256]{1,0:T(8,128)(2,1)S(1)}, u32[]{:S(2)}, u32[]{:S(2)}) %collective-permute-start.24) | collective-permute-done | bytes 131104 | tf_op jit(solution)/shard_map/ppermute | solution.py:229
  73.4 1.9 %collective-permute-start.3 = (bf16[128,1152]{1,0:T(8,128)(2,1)}, bf16[128,1152]{1,0:T(8,128)(2,1)S(1)}, u32[]{:S(2)}, u32[]{:S(2)}) collective-permute-start(bf16[128,1152]{1,0:T(8,128)(2,1)} %get-tuple-element.34), channel_id=1, source_target_pairs={{1,0},{0,1},{3,2},{2,3},{5,4},{4,5},{7,6},{6,7},{9,8},{8,9},{11,10... | collective-permute-start | bytes 884744 | tf_op jit(solution)/shard_map/ppermute | solution.py:222
  75.4 4.0 %collective-permute-done.4.refs_2_ = bf16[128,384]{1,0:T(8,128)(2,1)S(1)} collective-permute-done((bf16[128,384]{1,0:T(8,128)(2,1)}, bf16[128,384]{1,0:T(8,128)(2,1)S(1)}, u32[]{:S(2)}, u32[]{:S(2)}) %collective-permute-start.4) | collective-permute-done | bytes 98336 | tf_op jit(solution)/shard_map/ppermute | solution.py:222
  79.4 1.5 %collective-permute-start.16 = (bf16[256,384]{1,0:T(8,128)(2,1)}, bf16[256,384]{1,0:T(8,128)(2,1)S(1)}, u32[]{:S(2)}, u32[]{:S(2)}) collective-permute-start(bf16[256,384]{1,0:T(8,128)(2,1)} %get-tuple-element.48.refs_4_), channel_id=1, source_target_pairs={{0,8},{4,12},{8,0},{12,4},{16,24},{20,28},{24,16},{28,20},{1,9},{5... | collective-permute-start | bytes 589832 | tf_op jit(solution)/shard_map/ppermute | solution.py:229
  81.4 1.5 %collective-permute-start.18 = (bf16[256,384]{1,0:T(8,128)(2,1)}, bf16[256,384]{1,0:T(8,128)(2,1)S(1)}, u32[]{:S(2)}, u32[]{:S(2)}) collective-permute-start(bf16[256,384]{1,0:T(8,128)(2,1)} %get-tuple-element.48.refs_4_), channel_id=1, source_target_pairs={{0,24},{4,28},{8,16},{12,20},{16,8},{20,12},{24,0},{28,4},{1,25},{... | collective-permute-start | bytes 589832 | tf_op jit(solution)/shard_map/ppermute | solution.py:229
  82.9 2.0 %collective-permute-start.5 = (bf16[128,384]{1,0:T(8,128)(2,1)}, bf16[128,384]{1,0:T(8,128)(2,1)S(1)}, u32[]{:S(2)}, u32[]{:S(2)}) collective-permute-start(bf16[128,384]{1,0:T(8,128)(2,1)} %get-tuple-element.36), channel_id=1, source_target_pairs={{3,0},{2,1},{1,2},{0,3},{7,4},{6,5},{5,6},{4,7},{11,8},{10,9},{9,1... | collective-permute-start | bytes 294920 | tf_op jit(solution)/shard_map/ppermute | solution.py:222
  85.7 2.9 %shard_map.108 = (f32[320,256]{1,0:T(8,128)}, bf16[320,256]{1,0:T(8,128)(2,1)}) custom-call(bf16[256,640]{1,0:T(8,128)(2,1)} %pad_maximum_fusion.refs_0_, bf16[256,640]{1,0:T(8,128)(2,1)} %copy-done, bf16[256,640]{1,0:T(8,128)(2,1)} %copy-done.1, bf16[256,640]{1,0:T(8,128)(2,1)} %copy-done.2, bf16[256,256]{1,0:T(8,128)(2,1)} %get-tuple-element.51.refs_4_, ...), custom_call_target="tpu_custom_call" | custom-call | flops 335544320 | bytes 2326528 | tf_op jit(solution)/shard_map/pallas_call | solution.py:188
  90.3 2.4 %shard_map.106 = (bf16[128,1280]{1,0:T(8,128)(2,1)}, bf16[128,1280]{1,0:T(8,128)(2,1)}, bf16[128,1280]{1,0:T(8,128)(2,1)}) custom-call(bf16[128,1152]{1,0:T(8,128)(2,1)} %get-tuple-element.33.refs_0_, bf16[128,1152]{1,0:T(8,128)(2,1)} %copy-done.6, bf16[128,384]{1,0:T(8,128)(2,1)} %copy-done.15, bf16[128,384]{1,0:T(8,128)(2,1)} %copy-done.16, ...), custom_call_target="tpu_custom_call" | custom-call | bytes 2293760 | tf_op jit(solution)/shard_map/pallas_call | solution.py:188
  94.1 3.3 %shard_map.107 = (f32[320,384]{1,0:T(8,128)}, bf16[320,384]{1,0:T(8,128)(2,1)}) custom-call(bf16[256,640]{1,0:T(8,128)(2,1)} %pad_maximum_fusion.refs_0_, bf16[256,640]{1,0:T(8,128)(2,1)} %copy-done, bf16[256,640]{1,0:T(8,128)(2,1)} %copy-done.1, bf16[256,640]{1,0:T(8,128)(2,1)} %copy-done.2, bf16[256,384]{1,0:T(8,128)(2,1)} %get-tuple-element.48.refs_4_, ...), custom_call_target="tpu_custom_call" | custom-call | flops 503316480 | bytes 2834432 | tf_op jit(solution)/shard_map/pallas_call | solution.py:188
  99.5 4.2 %collective-permute-start.21 = (bf16[320,192]{1,0:T(8,128)(2,1)S(1)}, bf16[320,192]{1,0:T(8,128)(2,1)S(1)}, u32[]{:S(2)}, u32[]{:S(2)}) collective-permute-start(bf16[320,192]{1,0:T(8,128)(2,1)S(1)} %get-tuple-element.67), channel_id=1, source_target_pairs={{0,1},{1,3},{2,0},{3,2},{4,5},{5,7},{6,4},{7,6},{8,9},{9,11},{10,8... | collective-permute-start | bytes 368648 | tf_op jit(solution)/shard_map/ppermute | solution.py:293
  104.5 6.3 %collective-permute-done.21 = bf16[320,192]{1,0:T(8,128)(2,1)S(1)} collective-permute-done((bf16[320,192]{1,0:T(8,128)(2,1)S(1)}, bf16[320,192]{1,0:T(8,128)(2,1)S(1)}, u32[]{:S(2)}, u32[]{:S(2)}) %collective-permute-start.21) | collective-permute-done | bytes 122912 | tf_op jit(solution)/shard_map/ppermute | solution.py:293
  (97 shorter events, 14.4 us)
Async XLA Ops:
  0.6 39.5 %collective-permute-start.12 = (bf16[1,128,2560]{2,1,0:T(8,128)(2,1)}, bf16[1,128,2560]{2,1,0:T(8,128)(2,1)S(1)}, u32[]{:S(2)}, u32[]{:S(2)}) collective-permute-start(bf16[1,128,2560]{2,1,0:T(8,128)(2,1)} %param.7), channel_id=1, source_target_pairs={{0,1},{1,0},{2,3},{3,2},{4,5},{5,4},{6,7},{7,6},{8,9},{9,8},{10,11... | collective-permute-start | bytes 1966088 | tf_op jit(solution)/shard_map/ppermute | solution.py:219
  7.5 27.4 %collective-permute-start.6 = (bf16[1040,128]{1,0:T(8,128)(2,1)}, bf16[1040,128]{1,0:T(8,128)(2,1)S(1)}, u32[]{:S(2)}, u32[]{:S(2)}) collective-permute-start(bf16[1040,128]{1,0:T(8,128)(2,1)} %get-tuple-element.38), channel_id=1, source_target_pairs={{0,1},{1,0},{2,3},{3,2},{4,5},{5,4},{6,7},{7,6},{8,9},{9,8},{10,11... | collective-permute-start | bytes 798728 | tf_op jit(solution)/shard_map/ppermute | solution.py:219
  7.6 20.2 %collective-permute-start.7 = (bf16[528,128]{1,0:T(8,128)(2,1)}, bf16[528,128]{1,0:T(8,128)(2,1)S(1)}, u32[]{:S(2)}, u32[]{:S(2)}) collective-permute-start(bf16[528,128]{1,0:T(8,128)(2,1)} %get-tuple-element.39), channel_id=1, source_target_pairs={{0,2},{1,3},{2,0},{3,1},{4,6},{5,7},{6,4},{7,5},{8,10},{9,11},{10,... | collective-permute-start | bytes 405512 | tf_op jit(solution)/shard_map/ppermute | solution.py:219
  10.6 23.1 %collective-permute-start.8 = (bf16[528,128]{1,0:T(8,128)(2,1)}, bf16[528,128]{1,0:T(8,128)(2,1)}, u32[]{:S(2)}, u32[]{:S(2)}) collective-permute-start(bf16[528,128]{1,0:T(8,128)(2,1)} %get-tuple-element.40), channel_id=1, source_target_pairs={{0,3},{1,2},{2,1},{3,0},{4,7},{5,6},{6,5},{7,4},{8,11},{9,10},{10,... | collective-permute-start | bytes 405512 | tf_op jit(solution)/shard_map/ppermute | solution.py:219
  14.7 46.7 %collective-permute-start = (bf16[1568,128]{1,0:T(8,128)(2,1)}, bf16[1568,128]{1,0:T(8,128)(2,1)S(1)}, u32[]{:S(2)}, u32[]{:S(2)}) collective-permute-start(bf16[1568,128]{1,0:T(8,128)(2,1)} %get-tuple-element.30), channel_id=1, source_target_pairs={{0,1},{1,0},{2,3},{3,2},{4,5},{5,4},{6,7},{7,6},{8,9},{9,8},{10,11... | collective-permute-start | bytes 1204232 | tf_op jit(solution)/shard_map/ppermute | solution.py:219
  15.0 13.5 %copy-start.20 = (bf16[800,128]{1,0:T(8,128)(2,1)S(1)}, bf16[800,128]{1,0:T(8,128)(2,1)}, u32[]{:S(2)}) copy-start(bf16[800,128]{1,0:T(8,128)(2,1)} %get-tuple-element.31) | copy-start | bytes 614404
  15.0 18.7 %copy-start.19 = (bf16[800,128]{1,0:T(8,128)(2,1)S(1)}, bf16[800,128]{1,0:T(8,128)(2,1)}, u32[]{:S(2)}) copy-start(bf16[800,128]{1,0:T(8,128)(2,1)} %get-tuple-element.32) | copy-start | bytes 614404
  28.4 15.2 %collective-permute-start.1 = (bf16[800,128]{1,0:T(8,128)(2,1)S(1)}, bf16[800,128]{1,0:T(8,128)(2,1)S(1)}, u32[]{:S(2)}, u32[]{:S(2)}) collective-permute-start(bf16[800,128]{1,0:T(8,128)(2,1)S(1)} %copy-done.20), channel_id=1, source_target_pairs={{0,2},{1,3},{2,0},{3,1},{4,6},{5,7},{6,4},{7,5},{8,10},{9,11},{10,... | collective-permute-start | bytes 614408 | tf_op jit(solution)/shard_map/ppermute | solution.py:219
  33.7 17.0 %collective-permute-start.2 = (bf16[800,128]{1,0:T(8,128)(2,1)S(1)}, bf16[800,128]{1,0:T(8,128)(2,1)}, u32[]{:S(2)}, u32[]{:S(2)}) collective-permute-start(bf16[800,128]{1,0:T(8,128)(2,1)S(1)} %copy-done.19), channel_id=1, source_target_pairs={{0,3},{1,2},{2,1},{3,0},{4,7},{5,6},{6,5},{7,4},{8,11},{9,10},{10,... | collective-permute-start | bytes 614408 | tf_op jit(solution)/shard_map/ppermute | solution.py:219
  38.6 19.7 %collective-permute-start.22 = (bf16[256,256]{1,0:T(8,128)(2,1)}, bf16[256,256]{1,0:T(8,128)(2,1)S(1)}, u32[]{:S(2)}, u32[]{:S(2)}) collective-permute-start(bf16[256,256]{1,0:T(8,128)(2,1)} %get-tuple-element.51.refs_4_), channel_id=1, source_target_pairs={{0,8},{4,12},{8,0},{12,4},{16,24},{20,28},{24,16},{28,20},{1,9},{5... | collective-permute-start | bytes 393224 | tf_op jit(solution)/shard_map/ppermute | solution.py:229
  40.1 19.7 %collective-permute-start.23 = (bf16[256,256]{1,0:T(8,128)(2,1)}, bf16[256,256]{1,0:T(8,128)(2,1)S(1)}, u32[]{:S(2)}, u32[]{:S(2)}) collective-permute-start(bf16[256,256]{1,0:T(8,128)(2,1)} %get-tuple-element.51.refs_4_), channel_id=1, source_target_pairs={{0,16},{4,20},{8,24},{12,28},{16,0},{20,4},{24,8},{28,12},{1,17},{... | collective-permute-start | bytes 393224 | tf_op jit(solution)/shard_map/ppermute | solution.py:229
  43.6 9.3 %collective-permute-start.10 = (bf16[128,256]{1,0:T(8,128)(2,1)S(1)}, bf16[128,256]{1,0:T(8,128)(2,1)}, u32[]{:S(2)}, u32[]{:S(2)}) collective-permute-start(bf16[128,256]{1,0:T(8,128)(2,1)S(1)} %copy-done.24), channel_id=1, source_target_pairs={{2,0},{3,1},{0,2},{1,3},{6,4},{7,5},{4,6},{5,7},{10,8},{11,9},{8,1... | collective-permute-start | bytes 196616 | tf_op jit(solution)/shard_map/ppermute | solution.py:222
  50.7 6.2 %collective-permute-start.11 = (bf16[128,256]{1,0:T(8,128)(2,1)S(1)}, bf16[128,256]{1,0:T(8,128)(2,1)}, u32[]{:S(2)}, u32[]{:S(2)}) collective-permute-start(bf16[128,256]{1,0:T(8,128)(2,1)S(1)} %copy-done.23), channel_id=1, source_target_pairs={{3,0},{2,1},{1,2},{0,3},{7,4},{6,5},{5,6},{4,7},{11,8},{10,9},{9,1... | collective-permute-start | bytes 196616 | tf_op jit(solution)/shard_map/ppermute | solution.py:222
  52.9 28.0 %collective-permute-start.13 = (bf16[256,640]{1,0:T(8,128)(2,1)S(1)}, bf16[256,640]{1,0:T(8,128)(2,1)S(1)}, u32[]{:S(2)}, u32[]{:S(2)}) collective-permute-start(bf16[256,640]{1,0:T(8,128)(2,1)S(1)} %pad_maximum_fusion.1), channel_id=1, source_target_pairs={{0,8},{4,12},{8,0},{12,4},{16,24},{20,28},{24,16},{28,20},{1,9},{5... | collective-permute-start | bytes 983048 | tf_op jit(solution)/shard_map/ppermute | solution.py:229
  56.8 24.6 %collective-permute-start.14 = (bf16[256,640]{1,0:T(8,128)(2,1)S(1)}, bf16[256,640]{1,0:T(8,128)(2,1)S(1)}, u32[]{:S(2)}, u32[]{:S(2)}) collective-permute-start(bf16[256,640]{1,0:T(8,128)(2,1)S(1)} %pad_maximum_fusion.2), channel_id=1, source_target_pairs={{0,16},{4,20},{8,24},{12,28},{16,0},{20,4},{24,8},{28,12},{1,17},{... | collective-permute-start | bytes 983048 | tf_op jit(solution)/shard_map/ppermute | solution.py:229
  58.4 24.5 %collective-permute-start.15 = (bf16[256,640]{1,0:T(8,128)(2,1)S(1)}, bf16[256,640]{1,0:T(8,128)(2,1)S(1)}, u32[]{:S(2)}, u32[]{:S(2)}) collective-permute-start(bf16[256,640]{1,0:T(8,128)(2,1)S(1)} %pad_maximum_fusion.3), channel_id=1, source_target_pairs={{0,24},{4,28},{8,16},{12,20},{16,8},{20,12},{24,0},{28,4},{1,25},{... | collective-permute-start | bytes 983048 | tf_op jit(solution)/shard_map/ppermute | solution.py:229
  59.8 13.6 %collective-permute-start.24 = (bf16[256,256]{1,0:T(8,128)(2,1)S(1)}, bf16[256,256]{1,0:T(8,128)(2,1)S(1)}, u32[]{:S(2)}, u32[]{:S(2)}) collective-permute-start(bf16[256,256]{1,0:T(8,128)(2,1)S(1)} %copy-done.11), channel_id=1, source_target_pairs={{0,24},{4,28},{8,16},{12,20},{16,8},{20,12},{24,0},{28,4},{1,25},{... | collective-permute-start | bytes 393224 | tf_op jit(solution)/shard_map/ppermute | solution.py:229
  62.1 11.3 %collective-permute-start.9 = (bf16[128,768]{1,0:T(8,128)(2,1)}, bf16[128,768]{1,0:T(8,128)(2,1)S(1)}, u32[]{:S(2)}, u32[]{:S(2)}) collective-permute-start(bf16[128,768]{1,0:T(8,128)(2,1)} %get-tuple-element.42), channel_id=1, source_target_pairs={{1,0},{0,1},{3,2},{2,3},{5,4},{4,5},{7,6},{6,7},{9,8},{8,9},{11,10... | collective-permute-start | bytes 589832 | tf_op jit(solution)/shard_map/ppermute | solution.py:222
  73.4 12.3 %copy-start.14 = (bf16[256,256]{1,0:T(8,128)(2,1)}, bf16[256,256]{1,0:T(8,128)(2,1)S(1)}, u32[]{:S(2)}) copy-start(bf16[256,256]{1,0:T(8,128)(2,1)S(1)} %collective-permute-done.24.refs_7_) | copy-start | bytes 393220
  73.4 6.0 %collective-permute-start.4 = (bf16[128,384]{1,0:T(8,128)(2,1)}, bf16[128,384]{1,0:T(8,128)(2,1)S(1)}, u32[]{:S(2)}, u32[]{:S(2)}) collective-permute-start(bf16[128,384]{1,0:T(8,128)(2,1)} %get-tuple-element.35), channel_id=1, source_target_pairs={{2,0},{3,1},{0,2},{1,3},{6,4},{7,5},{4,6},{5,7},{10,8},{11,9},{8,1... | collective-permute-start | bytes 294920 | tf_op jit(solution)/shard_map/ppermute | solution.py:222
  73.4 15.2 %copy-start.7 = (bf16[128,768]{1,0:T(8,128)(2,1)}, bf16[128,768]{1,0:T(8,128)(2,1)S(1)}, u32[]{:S(2)}) copy-start(bf16[128,768]{1,0:T(8,128)(2,1)S(1)} %collective-permute-done.9.refs_5_) | copy-start | bytes 589828
  73.4 16.1 %collective-permute-start.3 = (bf16[128,1152]{1,0:T(8,128)(2,1)}, bf16[128,1152]{1,0:T(8,128)(2,1)S(1)}, u32[]{:S(2)}, u32[]{:S(2)}) collective-permute-start(bf16[128,1152]{1,0:T(8,128)(2,1)} %get-tuple-element.34), channel_id=1, source_target_pairs={{1,0},{0,1},{3,2},{2,3},{5,4},{4,5},{7,6},{6,7},{9,8},{8,9},{11,10... | collective-permute-start | bytes 884744 | tf_op jit(solution)/shard_map/ppermute | solution.py:222
  79.4 13.3 %collective-permute-start.16 = (bf16[256,384]{1,0:T(8,128)(2,1)}, bf16[256,384]{1,0:T(8,128)(2,1)S(1)}, u32[]{:S(2)}, u32[]{:S(2)}) collective-permute-start(bf16[256,384]{1,0:T(8,128)(2,1)} %get-tuple-element.48.refs_4_), channel_id=1, source_target_pairs={{0,8},{4,12},{8,0},{12,4},{16,24},{20,28},{24,16},{28,20},{1,9},{5... | collective-permute-start | bytes 589832 | tf_op jit(solution)/shard_map/ppermute | solution.py:229
  80.9 11.8 %collective-permute-start.17 = (bf16[256,384]{1,0:T(8,128)(2,1)}, bf16[256,384]{1,0:T(8,128)(2,1)S(1)}, u32[]{:S(2)}, u32[]{:S(2)}) collective-permute-start(bf16[256,384]{1,0:T(8,128)(2,1)} %get-tuple-element.48.refs_4_), channel_id=1, source_target_pairs={{0,16},{4,20},{8,24},{12,28},{16,0},{20,4},{24,8},{28,12},{1,17},{... | collective-permute-start | bytes 589832 | tf_op jit(solution)/shard_map/ppermute | solution.py:229
  81.4 11.3 %collective-permute-start.18 = (bf16[256,384]{1,0:T(8,128)(2,1)}, bf16[256,384]{1,0:T(8,128)(2,1)S(1)}, u32[]{:S(2)}, u32[]{:S(2)}) collective-permute-start(bf16[256,384]{1,0:T(8,128)(2,1)} %get-tuple-element.48.refs_4_), channel_id=1, source_target_pairs={{0,24},{4,28},{8,16},{12,20},{16,8},{20,12},{24,0},{28,4},{1,25},{... | collective-permute-start | bytes 589832 | tf_op jit(solution)/shard_map/ppermute | solution.py:229
  82.9 6.6 %collective-permute-start.5 = (bf16[128,384]{1,0:T(8,128)(2,1)}, bf16[128,384]{1,0:T(8,128)(2,1)S(1)}, u32[]{:S(2)}, u32[]{:S(2)}) collective-permute-start(bf16[128,384]{1,0:T(8,128)(2,1)} %get-tuple-element.36), channel_id=1, source_target_pairs={{3,0},{2,1},{1,2},{0,3},{7,4},{6,5},{5,6},{4,7},{11,8},{10,9},{9,1... | collective-permute-start | bytes 294920 | tf_op jit(solution)/shard_map/ppermute | solution.py:222
  89.5 8.4 %collective-permute-start.25 = (bf16[320,256]{1,0:T(8,128)(2,1)}, bf16[320,256]{1,0:T(8,128)(2,1)S(1)}, u32[]{:S(2)}, u32[]{:S(2)}) collective-permute-start(bf16[320,256]{1,0:T(8,128)(2,1)} %get-tuple-element.53), channel_id=1, source_target_pairs={{0,4},{4,0},{8,12},{12,8},{16,20},{20,16},{24,28},{28,24},{1,5},{5... | collective-permute-start | bytes 491528 | tf_op jit(solution)/shard_map/ppermute | solution.py:283
  97.4 1.9 %collective-permute-start.19 = (bf16[320,384]{1,0:T(8,128)(2,1)}, bf16[320,384]{1,0:T(8,128)(2,1)S(1)}, u32[]{:S(2)}, u32[]{:S(2)}) collective-permute-start(bf16[320,384]{1,0:T(8,128)(2,1)} %get-tuple-element.50), channel_id=1, source_target_pairs={{0,4},{4,0},{8,12},{12,8},{16,20},{20,16},{24,28},{28,24},{1,5},{5... | collective-permute-start | bytes 737288 | tf_op jit(solution)/shard_map/ppermute | solution.py:283
  98.0 6.4 %collective-permute-start.27 = (bf16[320,128]{1,0:T(8,128)(2,1)S(1)}, bf16[320,128]{1,0:T(8,128)(2,1)S(1)}, u32[]{:S(2)}, u32[]{:S(2)}) collective-permute-start(bf16[320,128]{1,0:T(8,128)(2,1)S(1)} %get-tuple-element.69), channel_id=1, source_target_pairs={{0,1},{1,3},{2,0},{3,2},{4,5},{5,7},{6,4},{7,6},{8,9},{9,11},{10,8... | collective-permute-start | bytes 245768 | tf_op jit(solution)/shard_map/ppermute | solution.py:293
  98.1 6.4 %collective-permute-start.26 = (bf16[320,128]{1,0:T(8,128)(2,1)S(1)}, bf16[320,128]{1,0:T(8,128)(2,1)S(1)}, u32[]{:S(2)}, u32[]{:S(2)}) collective-permute-start(bf16[320,128]{1,0:T(8,128)(2,1)S(1)} %get-tuple-element.68), channel_id=1, source_target_pairs={{0,0},{1,2},{2,1},{3,3},{4,4},{5,6},{6,5},{7,7},{8,8},{9,10},{10,9... | collective-permute-start | bytes 245768 | tf_op jit(solution)/shard_map/ppermute | solution.py:293
  99.5 11.3 %collective-permute-start.21 = (bf16[320,192]{1,0:T(8,128)(2,1)S(1)}, bf16[320,192]{1,0:T(8,128)(2,1)S(1)}, u32[]{:S(2)}, u32[]{:S(2)}) collective-permute-start(bf16[320,192]{1,0:T(8,128)(2,1)S(1)} %get-tuple-element.67), channel_id=1, source_target_pairs={{0,1},{1,3},{2,0},{3,2},{4,5},{5,7},{6,4},{7,6},{8,9},{9,11},{10,8... | collective-permute-start | bytes 368648 | tf_op jit(solution)/shard_map/ppermute | solution.py:293
  103.7 7.0 %collective-permute-start.20 = (bf16[320,192]{1,0:T(8,128)(2,1)S(1)}, bf16[320,192]{1,0:T(8,128)(2,1)S(1)}, u32[]{:S(2)}, u32[]{:S(2)}) collective-permute-start(bf16[320,192]{1,0:T(8,128)(2,1)S(1)} %get-tuple-element.66), channel_id=1, source_target_pairs={{0,0},{1,2},{2,1},{3,3},{4,4},{5,6},{6,5},{7,7},{8,8},{9,10},{10,9... | collective-permute-start | bytes 368648 | tf_op jit(solution)/shard_map/ppermute | solution.py:293
  (21 other events, 75.1 us)
